TPU v7x, 32 devices: a whole 2x2x4 slice. The times are simulated.
32 devices in a mesh: expert: 8 (over z, x), tensor: 4 (over y, core).
Axes of the slice: x: 2, y: 2, z: 4, core: 2. Of those that a mesh axis runs over, the one named last changes fastest.
Arguments:
- tokens: bfloat16 [1024, 4096], P('expert', 'tensor'), may hold values from -6 to 6
- expert_ids: int32 [1024, 8], P('expert'), may hold values from 0 to 15, all different within a row; in each aligned block of 128 rows (0 to 127, 128 to 255, ...) at most 96 rows name the same one
- combine_weight: float32 [1024, 8], P('expert'), may hold values from 0.05 to 0.5
- gate_weight: bfloat16 [16, 4096, 1024], P('expert', 'tensor'), may hold values from -0.09375 to 0.09375
- up_weight: bfloat16 [16, 4096, 1024], P('expert', 'tensor'), may hold values from -0.09375 to 0.09375
- down_weight: bfloat16 [16, 1024, 4096], P('expert', None, 'tensor'), may hold values from -0.1875 to 0.1875
- out_cotangent: bfloat16 [1024, 4096], P('expert', 'tensor'), may hold values from -3 to 3
Outputs:
- mixed: bfloat16 [1024, 4096], P('expert', 'tensor')
- token_grad: bfloat16 [1024, 4096], P('expert', 'tensor')
- combine_grad: float32 [1024, 8], P('expert')
- gate_grad: bfloat16 [16, 4096, 1024], P('expert', 'tensor')
- up_grad: bfloat16 [16, 4096, 1024], P('expert', 'tensor')
- down_grad: bfloat16 [16, 1024, 4096], P('expert', None, 'tensor')
Inputs may be any that keep to these rules, and one draw needn't show every extreme that they name: `expert_ids`: each row names 8 different experts. Among the rows of one device no expert is named by more than 96 rows, a bound that some block reaches.
All inputs are finite; a program needn't handle non-finite values.
Results may differ from a plain program's by a relative error of at most 0.023.
Values may be sent and summed in bfloat16 or wider, within the bound.
A program may use at most 128 MiB of HBM per device.

v0:
```python
import jax
import jax.numpy as jnp
from jax import lax
from jax.sharding import PartitionSpec as P


def per_device(
    tokens, expert_ids, combine_weight, gate_weight, up_weight, down_weight, out_cotangent
):
    groups = lax.axis_size("expert")
    local_experts = gate_weight.shape[0]
    width_share = tokens.shape[1]
    hidden = gate_weight.shape[2]
    tok_rows = tokens.shape[0]
    top_count = expert_ids.shape[1]
    experts_all = local_experts * groups
    capacity = 3 * tok_rows * top_count // (2 * experts_all)
    pair_count = tok_rows * top_count
    slot_total = local_experts * groups * capacity
    share_rows = hidden // lax.axis_size("tensor")
    flat_ids = expert_ids.reshape(pair_count)
    onehot = (flat_ids[:, None] == jnp.arange(experts_all, dtype=jnp.int32)[None, :]).astype(
        jnp.int32
    )
    running = jnp.cumsum(onehot, axis=0)
    position = jnp.sum(running * onehot, axis=1) - 1
    slot_of_pair = flat_ids * capacity + position
    slot_pair = (
        jnp.full((experts_all * capacity,), pair_count, jnp.int32)
        .at[slot_of_pair]
        .set(jnp.arange(pair_count, dtype=jnp.int32))
    )
    filled = slot_pair < pair_count
    safe_pair = jnp.minimum(slot_pair, pair_count - 1)
    slot_token = safe_pair // top_count
    token_send = jnp.where(filled[:, None], tokens[slot_token], jnp.zeros((), jnp.bfloat16))
    token_send = token_send.reshape(groups, local_experts * capacity, width_share)
    slot_weight = jnp.where(filled, combine_weight.reshape(pair_count)[safe_pair], jnp.float32(0.0))
    grads_send = (slot_weight[:, None] * out_cotangent[slot_token].astype(jnp.float32)).astype(
        jnp.bfloat16
    )
    grads_send = grads_send.reshape(groups, local_experts * capacity, width_share)
    routed_raw = lax.all_to_all(token_send, "expert", split_axis=0, concat_axis=0, tiled=True)
    routed = routed_raw.reshape(groups, local_experts, capacity, width_share)
    gate_part = jnp.einsum(
        "secd,edk->kesc", routed, gate_weight, preferred_element_type=jnp.float32
    ).reshape(hidden, slot_total)
    up_part = jnp.einsum(
        "secd,edk->kesc", routed, up_weight, preferred_element_type=jnp.float32
    ).reshape(hidden, slot_total)
    totals = lax.psum(
        jnp.concatenate([gate_part, up_part], axis=1).astype(jnp.bfloat16), "tensor"
    ).astype(jnp.float32)
    gate_full = totals[:, :slot_total].reshape(hidden, local_experts, groups, capacity)
    up_full = totals[:, slot_total:].reshape(hidden, local_experts, groups, capacity)
    hidden_all = (jax.nn.silu(gate_full) * up_full).astype(jnp.bfloat16)
    own_rows = lax.dynamic_slice_in_dim(
        totals, lax.axis_index("tensor") * share_rows, share_rows, 0
    )
    gate_own = own_rows[:, :slot_total].reshape(share_rows, local_experts, groups, capacity)
    up_own = own_rows[:, slot_total:].reshape(share_rows, local_experts, groups, capacity)
    expert_out = jnp.einsum(
        "fesc,efd->secd", hidden_all, down_weight, preferred_element_type=jnp.float32
    ).astype(jnp.bfloat16)
    expert_out = expert_out.reshape(groups, local_experts * capacity, width_share)
    returned = lax.all_to_all(
        expert_out, "expert", split_axis=0, concat_axis=0, tiled=True
    ).reshape(experts_all * capacity, width_share)
    pair_out = returned[slot_of_pair].reshape(tok_rows, top_count, width_share).astype(jnp.float32)
    mixed = jnp.sum(pair_out * combine_weight[:, :, None], axis=1).astype(jnp.bfloat16)
    partial_dots = jnp.sum(pair_out * out_cotangent.astype(jnp.float32)[:, None, :], axis=2)
    combine_grad = lax.psum(partial_dots, "tensor")
    grads_raw = lax.all_to_all(grads_send, "expert", split_axis=0, concat_axis=0, tiled=True)
    incoming_gradient = grads_raw.reshape(groups, local_experts, capacity, width_share)
    hidden_state_cotangent = lax.psum_scatter(
        jnp.einsum(
            "secd,ekd->kesc", incoming_gradient, down_weight, preferred_element_type=jnp.float32
        )
        .reshape(lax.axis_size("tensor") * share_rows, slot_total)
        .astype(jnp.bfloat16),
        "tensor",
        scatter_dimension=0,
        tiled=True,
    ).astype(jnp.float32)
    hidden_state_cotangent = hidden_state_cotangent.reshape(
        share_rows, local_experts, groups, capacity
    )
    down_grad = jnp.einsum(
        "fesc,secd->efd", hidden_all, incoming_gradient, preferred_element_type=jnp.float32
    ).astype(jnp.bfloat16)
    sigma = jax.nn.sigmoid(gate_own)
    gate_diff = (hidden_state_cotangent * up_own * sigma * (1.0 + gate_own * (1.0 - sigma))).astype(
        jnp.bfloat16
    )
    up_diff = (hidden_state_cotangent * jax.nn.silu(gate_own)).astype(jnp.bfloat16)
    gate_diffs, up_diffs = (
        lax.all_gather(gate_diff, "tensor", axis=0, tiled=True),
        lax.all_gather(up_diff, "tensor", axis=0, tiled=True),
    )
    routed_grad = jnp.einsum(
        "fesc,edf->secd", gate_diffs, gate_weight, preferred_element_type=jnp.float32
    )
    routed_grad = routed_grad + jnp.einsum(
        "fesc,edf->secd", up_diffs, up_weight, preferred_element_type=jnp.float32
    )
    routed_grad = routed_grad.astype(jnp.bfloat16).reshape(
        groups, local_experts * capacity, width_share
    )
    grad_back = lax.all_to_all(
        routed_grad, "expert", split_axis=0, concat_axis=0, tiled=True
    ).reshape(experts_all * capacity, width_share)
    token_grad = jnp.sum(
        grad_back[slot_of_pair].reshape(tok_rows, top_count, width_share).astype(jnp.float32),
        axis=1,
    ).astype(jnp.bfloat16)
    gate_grad = jnp.einsum(
        "secd,fesc->edf", routed, gate_diffs, preferred_element_type=jnp.float32
    ).astype(jnp.bfloat16)
    up_grad = jnp.einsum(
        "secd,fesc->edf", routed, up_diffs, preferred_element_type=jnp.float32
    ).astype(jnp.bfloat16)
    return (mixed, token_grad, combine_grad, gate_grad, up_grad, down_grad)


def solution(mesh):
    placed = (
        P("expert", "tensor"),
        P("expert", None),
        P("expert", None),
        P("expert", "tensor", None),
        P("expert", "tensor", None),
        P("expert", None, "tensor"),
        P("expert", "tensor"),
    )
    return jax.shard_map(
        per_device,
        mesh=mesh,
        in_specs=placed,
        out_specs=(
            P("expert", "tensor"),
            P("expert", "tensor"),
            P("expert", None),
            P("expert", "tensor", None),
            P("expert", "tensor", None),
            P("expert", None, "tensor"),
        ),
        check_vma=False,
    )
```

profile of v0, /device:TPU:0, one launch (start us, length us, event | category | flops | bytes accessed | tf_op | source)
XLA Modules:
  0.0 478.4 jit_solution(15574865615111957846)
XLA Ops:
  8.9 4.5 reduce-window.6
  14.1 4.3 scatter_custom_fusion
  19.3 5.9 %gather_fusion.2 = f32[1536]{0:T(1024)S(1)} fusion(f32[1024]{0:T(1024)S(1)} %reshape.156, s32[2048]{0:T(1024)S(1)} %get-tuple-element.22), kind=kCustom, calls=%fused_computation.2 | custom fusion | bytes 18432 | tf_op jit(solution)/shard_map/gather | solution.py:38
  25.3 5.1 %gather_fusion = bf16[1536,1024]{1,0:T(8,128)(2,1)S(1)} fusion(bf16[128,1024]{1,0:T(8,128)(2,1)S(1)} %copy-done, s32[2048]{0:T(1024)S(1)} %get-tuple-element.23), kind=kCustom, calls=%fused_computation | custom fusion | bytes 6297600 | tf_op jit(solution)/shard_map/gather | solution.py:36
  32.3 7.4 %all-to-all-start = ((bf16[8,192,1024]{2,1,0:T(8,128)(2,1)}), bf16[8,192,1024]{2,1,0:T(8,128)(2,1)}, u32[]{:S(2)}, u32[]{:S(2)}) async-start(bf16[8,192,1024]{2,1,0:T(8,128)(2,1)} %broadcast_select_fusion), calls=%async_computation | async-start | bytes 6291456 | tf_op jit(solution)/shard_map/all_to_all | solution.py:43
  39.8 5.1 %gather_fusion.3 = bf16[1536,1024]{1,0:T(8,128)(2,1)S(1)} fusion(bf16[128,1024]{1,0:T(8,128)(2,1)S(1)} %copy-done.2, s32[2048]{0:T(1024)S(1)} %get-tuple-element.23), kind=kCustom, calls=%fused_computation.3 | custom fusion | bytes 6297600 | tf_op jit(solution)/shard_map/gather | solution.py:39
  47.1 63.4 %all-to-all-done = bf16[8,192,1024]{2,1,0:T(8,128)(2,1)} async-done(((bf16[8,192,1024]{2,1,0:T(8,128)(2,1)}), bf16[8,192,1024]{2,1,0:T(8,128)(2,1)}, u32[]{:S(2)}, u32[]{:S(2)}) %all-to-all-start) | async-done | bytes 3145760 | tf_op jit(solution)/shard_map/all_to_all | solution.py:43
  110.5 3.7 all-to-all-start.2
  114.2 6.7 %fusion.34 = bf16[2,8,96,1024]{3,2,1,0:T(8,128)(2,1)S(1)} fusion(bf16[2,1024,1024]{2,1,0:T(8,128)(2,1)} %param.11, bf16[8,2,96,1024]{3,2,1,0:T(8,128)(2,1)} %bitcast.5), kind=kOutput, calls=%fused_computation.41 | convolution fusion | flops 3222798336 | bytes 10485760 | tf_op jit(solution)/shard_map/secd,edk->kesc/dot_general | solution.py:48
  120.9 5.5 %fusion.29 = bf16[2,8,96,1024]{3,2,1,0:T(8,128)(2,1)S(1)} fusion(bf16[2,1024,1024]{2,1,0:T(8,128)(2,1)S(1)} %copy-done.5, bf16[8,2,96,1024]{3,2,1,0:T(8,128)(2,1)} %bitcast.5), kind=kOutput, calls=%fused_computation.40 | convolution fusion | flops 3222798336 | bytes 10485760 | tf_op jit(solution)/shard_map/secd,edk->kesc/dot_general | solution.py:45
  129.9 55.1 %all-to-all-done.2 = bf16[8,192,1024]{2,1,0:T(8,128)(2,1)S(1)} async-done(((bf16[8,192,1024]{2,1,0:T(8,128)(2,1)}), bf16[8,192,1024]{2,1,0:T(8,128)(2,1)S(1)}, u32[]{:S(2)}, u32[]{:S(2)}) %all-to-all-start.2) | async-done | bytes 3145760 | tf_op jit(solution)/shard_map/all_to_all | solution.py:73
  185.0 8.2 %fusion.24 = bf16[2,8,96,1024]{3,2,1,0:T(8,128)(2,1)} fusion(bf16[2,1024,1024]{2,1,0:T(8,128)(2,1)} %param.12, bf16[8,2,96,1024]{3,2,1,0:T(8,128)(2,1)S(1)} %bitcast.103), kind=kOutput, calls=%fused_computation.39 | convolution fusion | flops 3222798336 | bytes 10485760 | tf_op jit(solution)/shard_map/secd,ekd->kesc/dot_general | solution.py:76
  193.5 57.5 %all-reduce.2.cloned.1.call-done = bf16[1024,3072]{0,1:T(8,128)(2,1)} async-done(((bf16[1024,3072]{0,1:T(8,128)(2,1)}), bf16[1024,3072]{0,1:T(8,128)(2,1)}) %all-reduce.2.cloned.1.call-update) | async-done | bytes 6291472 | tf_op jit(solution)/shard_map/psum | solution.py:51
  250.9 4.3 convert_element_type.79
  256.7 35.2 %reduce-scatter.2.cloned.1.call-done = bf16[256,1536]{0,1:T(8,128)(2,1)} async-done(((bf16[1024,1536]{0,1:T(8,128)(2,1)}), bf16[256,1536]{0,1:T(8,128)(2,1)}) %reduce-scatter.2.cloned.1.call-update) | async-done | bytes 786448 | tf_op jit(solution)/shard_map/reduce_scatter | solution.py:75
  295.2 4.4 fusion.52
  301.7 7.1 %convert_bitcast_fusion = bf16[8,2,96,1024]{3,2,0,1:T(8,128)(2,1)S(1)} fusion(bf16[1024,2,8,96]{0,3,2,1:T(8,128)(2,1)S(1)} %multiply_convert_fusion, bf16[2,1024,1024]{2,1,0:T(8,128)(2,1)} %param.12), kind=kOutput, calls=%fused_computation.33 | convolution fusion | flops 3222798336 | bytes 10485760 | tf_op jit(solution)/shard_map/fesc,efd->secd/dot_general | solution.py:62
  310.8 5.9 %all-to-all-start.1 = ((bf16[8,192,1024]{2,1,0:T(8,128)(2,1)}), bf16[8,192,1024]{2,1,0:T(8,128)(2,1)S(1)}, u32[]{:S(2)}, u32[]{:S(2)}) async-start(bf16[8,192,1024]{2,1,0:T(8,128)(2,1)} %bitcast.98), calls=%async_computation.1 | async-start | bytes 6291456 | tf_op jit(solution)/shard_map/all_to_all | solution.py:66
  316.7 7.5 %all-gather.5.cloned.1.call-done = bf16[1024,2,8,96]{0,3,2,1:T(8,128)(2,1)} async-done(((bf16[256,2,8,96]{0,3,2,1:T(8,128)(2,1)}), bf16[1024,2,8,96]{0,3,2,1:T(8,128)(2,1)}) %all-gather.5.cloned.1.call-update) | async-done | bytes 3145744 | tf_op jit(solution)/shard_map/all_gather | solution.py:98
  324.2 9.4 %fusion.3 = f32[2,8,96,1024]{3,2,1,0:T(8,128)} fusion(bf16[1024,2,8,96]{0,3,2,1:T(8,128)(2,1)} %all-gather.5.cloned.1.call-done, bf16[2,1024,1024]{2,1,0:T(8,128)(2,1)} %param.11), kind=kOutput, calls=%fused_computation.18 | convolution fusion | flops 3221225472 | bytes 13631488 | tf_op jit(solution)/shard_map/fesc,edf->secd/dot_general | solution.py:103
  333.6 21.0 %all-gather.3.cloned.1.call-done = bf16[1024,2,8,96]{0,3,2,1:T(8,128)(2,1)} async-done(((bf16[256,2,8,96]{0,3,2,1:T(8,128)(2,1)}), bf16[1024,2,8,96]{0,3,2,1:T(8,128)(2,1)}) %all-gather.3.cloned.1.call-update) | async-done | bytes 3145744 | tf_op jit(solution)/shard_map/all_gather | solution.py:97
  354.6 8.4 %fusion.15 = bf16[8,2,96,1024]{3,2,0,1:T(8,128)(2,1)S(1)} fusion(f32[2,8,96,1024]{3,2,1,0:T(8,128)} %fusion.3, bf16[1024,2,8,96]{0,3,2,1:T(8,128)(2,1)} %all-gather.3.cloned.1.call-done, bf16[2,1024,1024]{2,1,0:T(8,128)(2,1)} %param.10), kind=kOutput, calls=%fused_computation.30 | convolution fusion | flops 3224371200 | bytes 16777216 | tf_op jit(solution)/shard_map/fesc,edf->secd/dot_general | solution.py:100
  364.9 22.4 %all-to-all-done.1 = bf16[8,192,1024]{2,1,0:T(8,128)(2,1)S(1)} async-done(((bf16[8,192,1024]{2,1,0:T(8,128)(2,1)}), bf16[8,192,1024]{2,1,0:T(8,128)(2,1)S(1)}, u32[]{:S(2)}, u32[]{:S(2)}) %all-to-all-start.1) | async-done | bytes 3145760 | tf_op jit(solution)/shard_map/all_to_all | solution.py:66
  387.3 4.4 all-to-all-start.3
  392.6 8.3 %bitcast_convert_fusion = bf16[2,1024,1024]{2,1,0:T(8,128)(2,1)} fusion(bf16[1024,2,8,96]{0,3,2,1:T(8,128)(2,1)} %copy-done.4, bf16[8,2,96,1024]{3,2,1,0:T(8,128)(2,1)} %bitcast.104), kind=kOutput, calls=%fused_computation.6 | convolution fusion | flops 3223322624 | bytes 10485760 | tf_op jit(solution)/shard_map/fesc,secd->efd/dot_general | solution.py:88
  400.9 5.3 %gather_fusion.1 = bf16[1024,1024]{1,0:T(8,128)(2,1)} fusion(bf16[1536,1024]{1,0:T(8,128)(2,1)S(1)} %bitcast.94, s32[1024]{0:T(1024)S(1)} %broadcast_clamp_fusion), kind=kCustom, calls=%fused_computation.1 | custom fusion | bytes 4198400 | tf_op jit(solution)/shard_map/gather | solution.py:69
  406.3 4.2 fusion.2
  410.5 11.7 %psum.15 = f32[128,8]{1,0:T(8,128)S(1)} all-reduce(f32[128,8]{1,0:T(8,128)S(1)} %get-tuple-element.12), channel_id=1, replica_groups=mesh['expert'=8,'tensor'=4] {'tensor'}, use_global_device_ids=true, to_apply=%region_9.10 | all-reduce | flops 1024 | bytes 8192 | tf_op jit(solution)/shard_map/psum | solution.py:72
  422.9 7.1 %bitcast_convert_fusion.1 = bf16[2,1024,1024]{2,1,0:T(8,128)(2,1)} fusion(bf16[8,2,96,1024]{3,2,1,0:T(8,128)(2,1)} %bitcast.5, bf16[1024,2,8,96]{0,3,2,1:T(8,128)(2,1)S(1)} %copy-done.6), kind=kOutput, calls=%fused_computation.7 | convolution fusion | flops 3223322624 | bytes 10485760 | tf_op jit(solution)/shard_map/secd,fesc->edf/dot_general | solution.py:119
  429.9 6.9 %bitcast_convert_fusion.2 = bf16[2,1024,1024]{2,1,0:T(8,128)(2,1)} fusion(bf16[8,2,96,1024]{3,2,1,0:T(8,128)(2,1)} %bitcast.5, bf16[1024,2,8,96]{0,3,2,1:T(8,128)(2,1)S(1)} %copy-done.7), kind=kOutput, calls=%fused_computation.8 | convolution fusion | flops 3223322624 | bytes 10485760 | tf_op jit(solution)/shard_map/secd,fesc->edf/dot_general | solution.py:116
  436.8 25.1 %all-to-all-done.3 = bf16[8,192,1024]{2,1,0:T(8,128)(2,1)} async-done(((bf16[8,192,1024]{2,1,0:T(8,128)(2,1)}), bf16[8,192,1024]{2,1,0:T(8,128)(2,1)}, u32[]{:S(2)}, u32[]{:S(2)}) %all-to-all-start.3) | async-done | bytes 3145760 | tf_op jit(solution)/shard_map/all_to_all | solution.py:109
  462.0 7.3 %gather_fusion.4 = bf16[1024,1024]{1,0:T(8,128)(2,1)S(1)} fusion(bf16[1536,1024]{1,0:T(8,128)(2,1)} %bitcast.35, s32[1024]{0:T(1024)S(1)} %broadcast_clamp_fusion), kind=kCustom, calls=%fused_computation.4 | custom fusion | bytes 4198400 | tf_op jit(solution)/shard_map/gather | solution.py:113
  (61 shorter events, 25.6 us)
Async XLA Ops:
  7.2 18.1 %copy-start = (bf16[128,1024]{1,0:T(8,128)(2,1)S(1)}, bf16[128,1024]{1,0:T(8,128)(2,1)}, u32[]{:S(2)}) copy-start(bf16[128,1024]{1,0:T(8,128)(2,1)} %param.7) | copy-start | bytes 786436
  32.3 7.5 %copy-start.2 = (bf16[128,1024]{1,0:T(8,128)(2,1)S(1)}, bf16[128,1024]{1,0:T(8,128)(2,1)}, u32[]{:S(2)}) copy-start(bf16[128,1024]{1,0:T(8,128)(2,1)} %param.13) | copy-start | bytes 786436
  32.3 78.2 %all-to-all-start = ((bf16[8,192,1024]{2,1,0:T(8,128)(2,1)}), bf16[8,192,1024]{2,1,0:T(8,128)(2,1)}, u32[]{:S(2)}, u32[]{:S(2)}) async-start(bf16[8,192,1024]{2,1,0:T(8,128)(2,1)} %broadcast_select_fusion), calls=%async_computation | async-start | bytes 6291456 | tf_op jit(solution)/shard_map/all_to_all | solution.py:43
  110.5 74.5 %all-to-all-start.2 = ((bf16[8,192,1024]{2,1,0:T(8,128)(2,1)}), bf16[8,192,1024]{2,1,0:T(8,128)(2,1)S(1)}, u32[]{:S(2)}, u32[]{:S(2)}) async-start(bf16[8,192,1024]{2,1,0:T(8,128)(2,1)} %fusion), calls=%async_computation.2 | async-start | bytes 6291456 | tf_op jit(solution)/shard_map/all_to_all | solution.py:73
  114.1 136.8 %all-reduce.2.cloned.1.call-start = ((), (), s32[]{:S(2)}) async-start(), calls=%async_computation.5 | async-start | bytes 12582912 | tf_op jit(solution)/shard_map/psum | solution.py:51
  114.2 6.7 %copy-start.5 = (bf16[2,1024,1024]{2,1,0:T(8,128)(2,1)S(1)}, bf16[2,1024,1024]{2,1,0:T(8,128)(2,1)}, u32[]{:S(2)}) copy-start(bf16[2,1024,1024]{2,1,0:T(8,128)(2,1)} %param.10) | copy-start | bytes 12582916
  129.8 162.2 %reduce-scatter.2.cloned.1.call-start = ((), (), s32[]{:S(2)}) async-start(), calls=%async_computation.6 | async-start | bytes 3932160 | tf_op jit(solution)/shard_map/reduce_scatter | solution.py:75
  185.0 8.2 %copy-start.3 = (bf16[8,192,1024]{2,1,0:T(8,128)(2,1)}, bf16[8,192,1024]{2,1,0:T(8,128)(2,1)S(1)}, u32[]{:S(2)}) copy-start(bf16[8,192,1024]{2,1,0:T(8,128)(2,1)S(1)} %all-to-all-done.2) | copy-start | bytes 9437188
  193.2 131.0 %all-gather.5.cloned.1.call-start = ((), (), s32[]{:S(2)}) async-start(), calls=%async_computation.8 | async-start | bytes 3932160 | tf_op jit(solution)/shard_map/all_gather | solution.py:98
  295.1 59.4 %all-gather.3.cloned.1.call-start = ((), (), s32[]{:S(2)}) async-start(), calls=%async_computation.7 | async-start | bytes 3932160 | tf_op jit(solution)/shard_map/all_gather | solution.py:97
  301.7 7.1 %copy-start.4 = (bf16[1024,2,8,96]{0,3,2,1:T(8,128)(2,1)}, bf16[1024,2,8,96]{0,3,2,1:T(8,128)(2,1)S(1)}, u32[]{:S(2)}) copy-start(bf16[1024,2,8,96]{0,3,2,1:T(8,128)(2,1)S(1)} %multiply_convert_fusion) | copy-start | bytes 9437188
  310.8 76.5 %all-to-all-start.1 = ((bf16[8,192,1024]{2,1,0:T(8,128)(2,1)}), bf16[8,192,1024]{2,1,0:T(8,128)(2,1)S(1)}, u32[]{:S(2)}, u32[]{:S(2)}) async-start(bf16[8,192,1024]{2,1,0:T(8,128)(2,1)} %bitcast.98), calls=%async_computation.1 | async-start | bytes 6291456 | tf_op jit(solution)/shard_map/all_to_all | solution.py:66
  387.3 74.7 %all-to-all-start.3 = ((bf16[8,192,1024]{2,1,0:T(8,128)(2,1)}), bf16[8,192,1024]{2,1,0:T(8,128)(2,1)}, u32[]{:S(2)}, u32[]{:S(2)}) async-start(bf16[8,192,1024]{2,1,0:T(8,128)(2,1)} %bitcast.97), calls=%async_computation.4 | async-start | bytes 6291456 | tf_op jit(solution)/shard_map/all_to_all | solution.py:109
  406.3 16.6 %copy-start.6 = (bf16[1024,2,8,96]{0,3,2,1:T(8,128)(2,1)S(1)}, bf16[1024,2,8,96]{0,3,2,1:T(8,128)(2,1)}, u32[]{:S(2)}) copy-start(bf16[1024,2,8,96]{0,3,2,1:T(8,128)(2,1)} %all-gather.5.cloned.1.call-done) | copy-start | bytes 9437188
  422.9 7.1 %copy-start.7 = (bf16[1024,2,8,96]{0,3,2,1:T(8,128)(2,1)S(1)}, bf16[1024,2,8,96]{0,3,2,1:T(8,128)(2,1)}, u32[]{:S(2)}) copy-start(bf16[1024,2,8,96]{0,3,2,1:T(8,128)(2,1)} %all-gather.3.cloned.1.call-done) | copy-start | bytes 9437188
  462.0 9.4 %copy-start.1 = (bf16[128,1024]{1,0:T(8,128)(2,1)S(1)}, bf16[128,1024]{1,0:T(8,128)(2,1)}, u32[]{:S(2)}) copy-start(bf16[128,1024]{1,0:T(8,128)(2,1)} %param.7) | copy-start | bytes 786436
Sparse Core Ops, SparseCore 0:
  130.0 120.9 all-reduce.1
  254.0 37.8 reduce-scatter.1
  295.3 28.9 all-gather.4
  325.6 28.8 all-gather.2
where the time goes:
time: 487 us; the launch traced here: 478 us
  waiting for transfers between devices  287 us (59%)
  matrix products  67.5 us (14%)
  local copies, waits for them, and re-layouts  46 us (9%)
  other arithmetic  29.6 us (6%)
  starting transfers between devices  21.7 us (4%)
  between operations  14.5 us (3%)
  blocking collectives  11.7 us (2%)
    all_to_all x1, waiting for transfers between devices, per_device(): lax.all_to_all(token_send, 'expert', split_axis=0, concat_axis=0, tiled=T...  63.4 us
    psum x1, waiting for transfers between devices, per_device(): lax.psum(jnp.concatenate([gate_part, up_part], axis=1).astype(jnp.bfloat1...  57.5 us
    all_to_all x1, waiting for transfers between devices, per_device(): lax.all_to_all(grads_send, 'expert', split_axis=0, concat_axis=0, tiled=T...  55.1 us
    reduce_scatter x1, waiting for transfers between devices, per_device(): lax.psum_scatter(jnp.einsum('secd,ekd->kesc', incoming_gradient, down_wei...  35.2 us
    all_to_all x1, waiting for transfers between devices, per_device(): lax.all_to_all(routed_grad, 'expert', split_axis=0, concat_axis=0, tiled=...  25.1 us
    all_to_all x1, waiting for transfers between devices, per_device(): lax.all_to_all(expert_out, 'expert', split_axis=0, concat_axis=0, tiled=T...  22.4 us
    all_gather x1, waiting for transfers between devices, per_device(): lax.all_gather(gate_diff, 'tensor', axis=0, tiled=True)  21 us
    psum x1, blocking collectives, per_device(): combine_grad = lax.psum(partial_dots, 'tensor')  11.7 us
  transfers between devices with their start and end apart: 8, of which 8 were waited for; matrix products, arithmetic and copies ran while one was open for 22% of the time, Pallas kernels for 0%

commit v1 on v0

v1 whole, which is shorter than its diff:
```python
import jax
import jax.numpy as jnp
from jax import lax
from jax.sharding import PartitionSpec as P

F32, BF16 = jnp.float32, jnp.bfloat16


def dot(form, left, right):
    return jnp.einsum(form, left, right, preferred_element_type=F32)


def per_device(
    tokens, expert_ids, combine_weight, gate_weight, up_weight, down_weight, out_cotangent
):
    groups = lax.axis_size("expert")
    shards = lax.axis_size("tensor")
    local = gate_weight.shape[0]
    width = tokens.shape[1]
    hidden = gate_weight.shape[2]
    rows = tokens.shape[0]
    top = expert_ids.shape[1]
    experts = local * groups
    capacity = 3 * rows * top // (2 * experts)
    slots = groups * capacity
    total = local * slots
    own = total // shards
    mine = lax.axis_index("expert")

    named = expert_ids[:, :, None] == jnp.arange(experts, dtype=jnp.int32)
    dense_weight = jnp.sum(jnp.where(named, combine_weight[:, :, None], 0.0), axis=1)
    weights_all = lax.all_gather(dense_weight, "expert", axis=0)
    tokens_all = lax.all_gather(tokens, "expert", axis=0)
    cotangent_all = lax.all_gather(out_cotangent, "expert", axis=0)
    weight_tok = lax.dynamic_slice_in_dim(weights_all, mine * local, local, 2)
    weight_tok = weight_tok.transpose(2, 0, 1)
    served = weight_tok > 0.0
    earlier = (jnp.arange(rows)[:, None] < jnp.arange(rows)[None, :]).astype(BF16)
    position = dot("ebs,st->ebt", served.astype(BF16), earlier)
    at_slot = jnp.where(served, position, -1.0).astype(jnp.int32)
    chosen = at_slot[:, :, None, :] == jnp.arange(capacity, dtype=jnp.int32)[:, None]
    place = chosen.astype(BF16)
    weight_slot = jnp.sum(jnp.where(chosen, weight_tok[:, :, None, :], 0.0), axis=3)
    weight_slot = weight_slot.reshape(total, 1)
    weight_own = lax.dynamic_slice_in_dim(
        weight_slot, lax.axis_index("tensor") * own, own, 0
    )

    def dispatch(values):
        return [
            dot("bct,btd->bcd", place[e], values).astype(BF16).reshape(slots, width)
            for e in range(local)
        ]

    def scatter_rows(parts):
        return lax.psum_scatter(
            jnp.concatenate(parts, axis=0), "tensor", scatter_dimension=0, tiled=True
        ).astype(F32)

    def gather_rows(value):
        full = lax.all_gather(value.astype(BF16), "tensor", axis=0, tiled=True)
        return full.reshape(local, slots, hidden)

    def combine(parts):
        total_sum = sum(
            dot("bct,bcd->btd", place[e], parts[e].reshape(groups, capacity, width))
            for e in range(local)
        )
        return lax.psum_scatter(
            total_sum.astype(BF16), "expert", scatter_dimension=0, tiled=True
        ).reshape(rows, width)

    routed = dispatch(tokens_all)
    gate = scatter_rows(
        [dot("cd,dk->ck", routed[e], gate_weight[e]).astype(BF16) for e in range(local)]
    )
    up = scatter_rows(
        [dot("cd,dk->ck", routed[e], up_weight[e]).astype(BF16) for e in range(local)]
    )
    incoming = dispatch(cotangent_all)
    pulled = scatter_rows(
        [dot("cd,kd->ck", incoming[e], down_weight[e]).astype(BF16) for e in range(local)]
    )
    sigma = jax.nn.sigmoid(gate)
    silu = gate * sigma
    act = silu * up
    weighted_act = gather_rows(weight_own * act)
    weighted_pull = weight_own * pulled
    gate_diff = gather_rows(weighted_pull * up * sigma * (1.0 + gate * (1.0 - sigma)))
    up_diff = gather_rows(weighted_pull * silu)

    pair_own = jnp.sum(act * pulled, axis=1)
    pair_all = lax.all_gather(pair_own, "tensor", axis=0, tiled=True)
    pair_all = pair_all.reshape(local, groups, capacity)
    pair_tok = jnp.sum(jnp.where(chosen, pair_all[:, :, :, None], 0.0), axis=2)
    pair_tok = lax.all_to_all(
        pair_tok.transpose(1, 0, 2), "expert", split_axis=0, concat_axis=0, tiled=True
    ).reshape(experts, rows)
    combine_grad = jnp.sum(jnp.where(named, pair_tok.T[:, None, :], 0.0), axis=2)

    mixed = combine(
        [
            dot("ck,kd->cd", weighted_act[e], down_weight[e]).astype(BF16)
            for e in range(local)
        ]
    )
    token_grad = combine(
        [
            (
                dot("ck,dk->cd", gate_diff[e], gate_weight[e])
                + dot("ck,dk->cd", up_diff[e], up_weight[e])
            ).astype(BF16)
            for e in range(local)
        ]
    )
    down_grad = jnp.stack(
        [dot("ck,cd->kd", weighted_act[e], incoming[e]).astype(BF16) for e in range(local)]
    )
    gate_grad = jnp.stack(
        [dot("cd,ck->dk", routed[e], gate_diff[e]).astype(BF16) for e in range(local)]
    )
    up_grad = jnp.stack(
        [dot("cd,ck->dk", routed[e], up_diff[e]).astype(BF16) for e in range(local)]
    )
    return (mixed, token_grad, combine_grad, gate_grad, up_grad, down_grad)


def solution(mesh):
    wide, narrow = P("expert", "tensor"), P("expert", None)
    deep, flat = P("expert", "tensor", None), P("expert", None, "tensor")
    return jax.shard_map(
        per_device,
        mesh=mesh,
        in_specs=(wide, narrow, narrow, deep, deep, flat, wide),
        out_specs=(wide, wide, narrow, deep, deep, flat),
        check_vma=False,
    )
```

time: 487 us -> 493 us (1.012)
  waiting for transfers between devices: 287 us -> 336 us
  blocking collectives: 11.7 us -> 50 us
  local copies, waits for them, and re-layouts: 46 us -> 8.36 us
  starting transfers between devices: 21.7 us -> 0.78 us
  matrix products: 67.5 us -> 54.6 us
  other arithmetic: 29.6 us -> 20.2 us
    all_to_all x4 -> x0, waiting for transfers between devices: 166 us -> none  [the longest x1 63.4 us: per_device(): lax.all_to_all(token_send, 'expert', split_axis=0, concat_axis=0, tiled=T...]
    reduce_scatter x1 -> x5, waiting for transfers between devices: 35.2 us -> 199 us  [the longest x3 104 us: scatter_rows(): lax.psum_scatter(jnp.concatenate(parts, axis=0), 'tensor', scatter_dimens...]
    all_gather x2 -> x5, waiting for transfers between devices: 28.5 us -> 135 us  [the longest x3 74.2 us: gather_rows(): full = lax.all_gather(value.astype(BF16), 'tensor', axis=0, tiled=True)]
    psum x1 -> x0, waiting for transfers between devices: 57.5 us -> none  [per_device(): lax.psum(jnp.concatenate([gate_part, up_part], axis=1).astype(jnp.bfloat1...]
    all_gather x0 -> x2, blocking collectives: none -> 37.7 us  [the longest x1 32.6 us: per_device(): weights_all = lax.all_gather(dense_weight, 'expert', axis=0)]
    gather x5 -> x0, local copies, waits for them, and re-layouts: 28.6 us -> none  [the longest x1 7.31 us: per_device(): grad_back[slot_of_pair].reshape(tok_rows, top_count, width_share)]
    all_to_all x4 -> x0, starting transfers between devices: 21.4 us -> none  [the longest x1 7.41 us: per_device(): lax.all_to_all(token_send, 'expert', split_axis=0, concat_axis=0, tiled=T...]
    dot_general x9 -> x27, matrix products: 67.5 us -> 54.6 us  [dot(): return jnp.einsum(form, left, right, preferred_element_type=F32)]
  transfers between devices with their start and end apart: 8 -> 10, of which waited for: 8 -> 10; matrix products, arithmetic and copies ran while one was open for 22% -> 14% of each run, Pallas kernels for 0% -> 0%
where the time goes in v1:
time: 493 us; the launch traced here: 485 us
  waiting for transfers between devices  336 us (68%)
  matrix products  54.6 us (11%)
  blocking collectives  50 us (10%)
  other arithmetic  20.2 us (4%)
  between operations  15 us (3%)
  local copies, waits for them, and re-layouts  8.36 us (2%)
    reduce_scatter x3, waiting for transfers between devices, scatter_rows(): lax.psum_scatter(jnp.concatenate(parts, axis=0), 'tensor', scatter_dimens...  104 us
    reduce_scatter x2, waiting for transfers between devices, combine(): lax.psum_scatter(total_sum.astype(BF16), 'expert', scatter_dimension=0, t...  95 us
    all_gather x3, waiting for transfers between devices, gather_rows(): full = lax.all_gather(value.astype(BF16), 'tensor', axis=0, tiled=True)  74.2 us
    dot_general x27, matrix products, dot(): return jnp.einsum(form, left, right, preferred_element_type=F32)  54.6 us
    all_gather x1, waiting for transfers between devices, per_device(): cotangent_all = lax.all_gather(out_cotangent, 'expert', axis=0)  40.4 us
    all_gather x1, blocking collectives, per_device(): weights_all = lax.all_gather(dense_weight, 'expert', axis=0)  32.6 us
    all_gather x1, waiting for transfers between devices, per_device(): tokens_all = lax.all_gather(tokens, 'expert', axis=0)  20 us
    all_to_all x1, blocking collectives, per_device(): lax.all_to_all(pair_tok.transpose(1, 0, 2), 'expert', split_axis=0, conca...  12.2 us
  transfers between devices with their start and end apart: 10, of which 10 were waited for; matrix products, arithmetic and copies ran while one was open for 14% of the time, Pallas kernels for 0%

profile of v1, /device:TPU:0, one launch (start us, length us, event | category | flops | bytes accessed | tf_op | source)
XLA Modules:
  0.0 485.4 jit_solution(2494550937460764869)
XLA Ops:
  9.4 32.6 %all-gather = f32[1024,16]{0,1:T(8,128)S(1)} all-gather(f32[128,16]{0,1:T(8,128)S(1)} %select_reduce_fusion.3), channel_id=2, replica_groups=mesh['expert'=8,'tensor'=4] {'expert'}, dimensions={0}, use_global_device_ids=true | all-gather | bytes 73728 | tf_op jit(solution)/shard_map/all_gather | solution.py:32
  42.3 20.0 %all-gather.16.cloned.1.call-done = bf16[1024,1024]{1,0:T(8,128)(2,1)} async-done(((bf16[128,1024]{1,0:T(8,128)(2,1)}), bf16[1024,1024]{1,0:T(8,128)(2,1)}) %all-gather.16.cloned.1.call-update) | async-done | bytes 2097168 | tf_op jit(solution)/shard_map/all_gather | solution.py:33
  62.3 2.3 convolution_convert_fusion.2
  69.6 2.0 pad_maximum_fusion.4
  71.7 40.4 %all-gather.18.cloned.1.call-done = bf16[1024,1024]{1,0:T(8,128)(2,1)} async-done(((bf16[128,1024]{1,0:T(8,128)(2,1)}), bf16[1024,1024]{1,0:T(8,128)(2,1)}) %all-gather.18.cloned.1.call-update) | async-done | bytes 2097168 | tf_op jit(solution)/shard_map/all_gather | solution.py:34
  112.1 2.3 convolution_convert_fusion
  119.5 2.0 pad_maximum_fusion.5
  121.7 3.7 fusion.40
  127.3 2.0 pad_maximum_fusion.3
  129.4 22.3 %reduce-scatter.8.cloned.1.call-done = bf16[384,1024]{1,0:T(8,128)(2,1)} async-done(((bf16[1536,1024]{1,0:T(8,128)(2,1)}), bf16[384,1024]{1,0:T(8,128)(2,1)}) %reduce-scatter.8.cloned.1.call-update) | async-done | bytes 786448 | tf_op jit(solution)/shard_map/reduce_scatter | solution.py:56
  151.6 40.9 %reduce-scatter.12.cloned.1.call-done = bf16[384,1024]{1,0:T(8,128)(2,1)} async-done(((bf16[1536,1024]{1,0:T(8,128)(2,1)}), bf16[384,1024]{1,0:T(8,128)(2,1)}) %reduce-scatter.12.cloned.1.call-update) | async-done | bytes 786448 | tf_op jit(solution)/shard_map/reduce_scatter | solution.py:56
  192.5 40.9 %reduce-scatter.6.cloned.1.call-done = bf16[384,1024]{1,0:T(8,128)(2,1)} async-done(((bf16[1536,1024]{1,0:T(8,128)(2,1)}), bf16[384,1024]{1,0:T(8,128)(2,1)}) %reduce-scatter.6.cloned.1.call-update) | async-done | bytes 786448 | tf_op jit(solution)/shard_map/reduce_scatter | solution.py:56
  233.4 2.3 fusion.65
  235.7 5.2 %all-gather.3 = f32[4,1,384]{2,1,0:T(1,128)S(1)} all-gather(f32[1,1,384]{2,1,0:T(1,128)S(1)} %reshape.84), channel_id=1, replica_groups=mesh['expert'=8,'tensor'=4] {'tensor'}, dimensions={0}, use_global_device_ids=true | all-gather | bytes 7680 | tf_op jit(solution)/shard_map/all_gather | solution.py:93
  241.8 2.6 fusion.64
  245.9 27.1 %all-gather.10.cloned.1.call-done = bf16[1536,1024]{1,0:T(8,128)(2,1)} async-done(((bf16[384,1024]{1,0:T(8,128)(2,1)}), bf16[1536,1024]{1,0:T(8,128)(2,1)}) %all-gather.10.cloned.1.call-update) | async-done | bytes 3145744 | tf_op jit(solution)/shard_map/all_gather | solution.py:61
  273.0 4.0 fusion.49
  281.0 2.1 add_convert_fusion.1
  283.4 20.3 %all-gather.14.cloned.1.call-done = bf16[1536,1024]{1,0:T(8,128)(2,1)} async-done(((bf16[384,1024]{1,0:T(8,128)(2,1)}), bf16[1536,1024]{1,0:T(8,128)(2,1)}) %all-gather.14.cloned.1.call-update) | async-done | bytes 3145744 | tf_op jit(solution)/shard_map/all_gather | solution.py:61
  303.7 3.9 fusion.12
  307.6 26.8 %all-gather.12.cloned.1.call-done = bf16[1536,1024]{1,0:T(8,128)(2,1)} async-done(((bf16[384,1024]{1,0:T(8,128)(2,1)}), bf16[1536,1024]{1,0:T(8,128)(2,1)}) %all-gather.12.cloned.1.call-update) | async-done | bytes 3145744 | tf_op jit(solution)/shard_map/all_gather | solution.py:61
  334.4 4.1 add_convert_fusion.3
  345.6 2.2 add_convert_fusion
  347.9 12.2 %all_to_all.5 = f32[8,2,128]{2,1,0:T(2,128)S(1)} all-to-all(f32[8,2,128]{2,1,0:T(2,128)S(1)} %copy.26), channel_id=1, replica_groups=mesh['expert'=8,'tensor'=4] {'expert'}, dimensions={0} | all-to-all | bytes 16384 | tf_op jit(solution)/shard_map/all_to_all | solution.py:96
  360.7 3.4 convert_bitcast_fusion.4
  364.2 1.9 convert_bitcast_fusion.5
  366.0 2.5 pad_maximum_fusion
  371.3 1.9 convert_bitcast_fusion.3
  373.2 2.5 pad_maximum_fusion.1
  380.8 2.4 pad_maximum_fusion.2
  383.2 23.7 %reduce-scatter.10.cloned.1.call-done = bf16[1,128,1024]{2,1,0:T(8,128)(2,1)} async-done(((bf16[8,128,1024]{2,1,0:T(8,128)(2,1)}), bf16[1,128,1024]{2,1,0:T(8,128)(2,1)}) %reduce-scatter.10.cloned.1.call-update) | async-done | bytes 262160 | tf_op jit(solution)/shard_map/reduce_scatter | solution.py:69
  406.9 71.3 %reduce-scatter.14.cloned.1.call-done = bf16[1,128,1024]{2,1,0:T(8,128)(2,1)} async-done(((bf16[8,128,1024]{2,1,0:T(8,128)(2,1)}), bf16[1,128,1024]{2,1,0:T(8,128)(2,1)}) %reduce-scatter.14.cloned.1.call-update) | async-done | bytes 262160 | tf_op jit(solution)/shard_map/reduce_scatter | solution.py:69
  (100 shorter events, 37.0 us)
Async XLA Ops:
  7.2 55.1 %all-gather.16.cloned.1.call-start = ((), (), s32[]{:S(2)}) async-start(), calls=%async_computation.14 | async-start | bytes 2359296 | tf_op jit(solution)/shard_map/all_gather | solution.py:33
  7.9 104.2 %all-gather.18.cloned.1.call-start = ((), (), s32[]{:S(2)}) async-start(), calls=%async_computation.15 | async-start | bytes 2359296 | tf_op jit(solution)/shard_map/all_gather | solution.py:34
  8.6 143.0 %reduce-scatter.8.cloned.1.call-start = ((), (), s32[]{:S(2)}) async-start(), calls=%async_computation.7 | async-start | bytes 3932160 | tf_op jit(solution)/shard_map/reduce_scatter | solution.py:56
  62.3 2.3 copy-start.1
  62.3 3.8 copy-start.16
  64.6 57.1 %copy-start.7 = (bf16[8,96,1024]{2,1,0:T(8,128)(2,1)}, bf16[8,96,1024]{2,1,0:T(8,128)(2,1)S(1)}, u32[]{:S(2)}) copy-start(bf16[8,96,1024]{2,1,0:T(8,128)(2,1)S(1)} %convolution_convert_fusion.2) | copy-start | bytes 4718596
  65.2 60.3 %copy-start.5 = (bf16[8,96,1024]{2,1,0:T(8,128)(2,1)}, bf16[8,96,1024]{2,1,0:T(8,128)(2,1)S(1)}, u32[]{:S(2)}) copy-start(bf16[8,96,1024]{2,1,0:T(8,128)(2,1)S(1)} %convolution_convert_fusion.3) | copy-start | bytes 4718596
  71.6 120.9 %reduce-scatter.12.cloned.1.call-start = ((), (), s32[]{:S(2)}) async-start(), calls=%async_computation.10 | async-start | bytes 3932160 | tf_op jit(solution)/shard_map/reduce_scatter | solution.py:56
  112.1 2.3 copy-start
  112.1 3.7 copy-start.14
  114.4 3.2 copy-start.11
  115.0 2.7 copy-start.9
  121.5 111.9 %reduce-scatter.6.cloned.1.call-start = ((), (), s32[]{:S(2)}) async-start(), calls=%async_computation.6 | async-start | bytes 3932160 | tf_op jit(solution)/shard_map/reduce_scatter | solution.py:56
  121.7 3.8 copy-start.18
  129.3 143.7 %all-gather.10.cloned.1.call-start = ((), (), s32[]{:S(2)}) async-start(), calls=%async_computation.8 | async-start | bytes 3932160 | tf_op jit(solution)/shard_map/all_gather | solution.py:61
  151.6 90.1 %copy-start.2 = (bf16[384,1024]{1,0:T(8,128)(2,1)S(1)}, bf16[384,1024]{1,0:T(8,128)(2,1)}, u32[]{:S(2)}) copy-start(bf16[384,1024]{1,0:T(8,128)(2,1)} %reduce-scatter.8.cloned.1.call-done) | copy-start | bytes 2359300
  192.5 49.2 %copy-start.3 = (bf16[384,1024]{1,0:T(8,128)(2,1)S(1)}, bf16[384,1024]{1,0:T(8,128)(2,1)}, u32[]{:S(2)}) copy-start(bf16[384,1024]{1,0:T(8,128)(2,1)} %reduce-scatter.12.cloned.1.call-done) | copy-start | bytes 2359300
  233.4 8.3 %copy-start.4 = (bf16[384,1024]{1,0:T(8,128)(2,1)S(1)}, bf16[384,1024]{1,0:T(8,128)(2,1)}, u32[]{:S(2)}) copy-start(bf16[384,1024]{1,0:T(8,128)(2,1)} %reduce-scatter.6.cloned.1.call-done) | copy-start | bytes 2359300
  244.3 59.3 %all-gather.14.cloned.1.call-start = ((), (), s32[]{:S(2)}) async-start(), calls=%async_computation.12 | async-start | bytes 3932160 | tf_op jit(solution)/shard_map/all_gather | solution.py:61
  245.1 89.3 %all-gather.12.cloned.1.call-start = ((), (), s32[]{:S(2)}) async-start(), calls=%async_computation.11 | async-start | bytes 3932160 | tf_op jit(solution)/shard_map/all_gather | solution.py:61
  245.8 161.0 %reduce-scatter.10.cloned.1.call-start = ((), (), s32[]{:S(2)}) async-start(), calls=%async_computation.9 | async-start | bytes 2359296 | tf_op jit(solution)/shard_map/reduce_scatter | solution.py:69
  273.0 4.8 copy-start.20
  283.1 195.0 %reduce-scatter.14.cloned.1.call-start = ((), (), s32[]{:S(2)}) async-start(), calls=%async_computation.13 | async-start | bytes 2359296 | tf_op jit(solution)/shard_map/reduce_scatter | solution.py:69
  334.3 4.9 copy-start.22
  340.6 3.2 copy-start.24
  347.8 12.3 %copy-start.13 = (s32[128,8]{0,1:T(8,128)S(1)}, s32[128,8]{0,1:T(8,128)}, u32[]{:S(2)}) copy-start(s32[128,8]{0,1:T(8,128)} %param.8) | copy-start | bytes 12292
  347.8 12.9 %copy-start.8 = (bf16[8,96,1024]{2,1,0:T(8,128)(2,1)S(1)}, bf16[8,96,1024]{2,1,0:T(8,128)(2,1)}, u32[]{:S(2)}) copy-start(bf16[8,96,1024]{2,1,0:T(8,128)(2,1)} %copy-done.7) | copy-start | bytes 4718596
  360.7 3.4 copy-start.6
  360.7 3.4 copy-start.25
  366.0 3.4 copy-start.23
  373.2 2.5 copy-start.12
  373.2 3.9 copy-start.21
  (4 other events, 8.4 us)
Sparse Core Ops, SparseCore 0:
  10.1 52.1 all-gather.15
  64.4 47.6 all-gather.17
  115.2 36.3 reduce-scatter.7
  154.6 37.9 reduce-scatter.11
  195.5 37.8 reduce-scatter.5
  244.5 28.4 all-gather.9
  275.1 28.4 all-gather.13
  305.8 28.4 all-gather.11
  338.5 68.3 reduce-scatter.9
  410.8 67.2 reduce-scatter.13
